TPU v7x, 256 devices: a whole 4x4x8 slice. The times are simulated.
256 devices in a mesh: cfg: 2 (over x_hi), seq: 64 (over x_lo, z, y), clip: 2 (over core).
Axes of the slice: x: 4 (x_hi: 2, x_lo: 2; x = x_hi * 2 + x_lo), y: 4, z: 8, core: 2. Of those that a mesh axis runs over, the one named last changes fastest.
Arguments:
- clean: bfloat16 [128, 256, 1152], P(('clip', 'seq')), parts along dimension 0, may hold values from -6 to 6
- noise: bfloat16 [128, 256, 1152], P(('clip', 'seq')), parts along dimension 0, may hold values from -6 to 6
- timestep: float32 [2], P('clip'), parts along dimension 0, may hold values from 0.1 to 0.9
- guidance: float32 [2], P('clip'), parts along dimension 0, may hold values from 2 to 6
- condition_vector: bfloat16 [2304], P('clip'), parts along dimension 0, may hold values from -6 to 6
- empty_prompt_vector: bfloat16 [1152], replicated, may hold values from -6 to 6
- timestep_direction: bfloat16 [1152], replicated, may hold values from -6 to 6
- spatial_query_key_value: bfloat16 [3, 1152, 1152], P(None, None, ('cfg', 'seq')), may hold values from -1 to 1
- spatial_output_weight: bfloat16 [1152, 1152], P(('cfg', 'seq')), may hold values from -0.1875 to 0.1875
- temporal_query_key_value: bfloat16 [3, 1152, 1152], P(None, None, ('cfg', 'seq')), may hold values from -1 to 1
- temporal_output_weight: bfloat16 [1152, 1152], P(('cfg', 'seq')), may hold values from -0.1875 to 0.1875
- adapter_down_maps: bfloat16 [2, 1152, 64], replicated, may hold values from -0.1875 to 0.1875
- adapter_up_maps: bfloat16 [2, 64, 1152], replicated, may hold values from -0.75 to 0.75
Outputs:
- student_out: bfloat16 [128, 256, 1152], P(('clip', 'seq'), 'cfg'), parts along dimension 0
- student_tangent: bfloat16 [128, 256, 1152], P(('clip', 'seq'), 'cfg'), parts along dimension 0
There are 2 independent parts, one for each index of `clip`. A program takes and returns all parts, laid end to end along the dimension named above; an argument that names none is the same for every part. Nothing has to cross between parts.
All inputs are finite; a program needn't handle non-finite values.
Results may differ from a plain program's by a relative error of at most 0.028.
Values may be sent and summed in bfloat16 or wider, within the bound.
A program may use at most 128 MiB of HBM per device.

v0:
```python
import jax
import jax.numpy as jnp
from jax import lax
from jax.sharding import PartitionSpec as P

HEAD_DIM = 72


epsilon = 1e-06


def partner(value, axis, bit):
    mask = 2**bit
    pairs = [(source, source ^ mask) for source in range(lax.axis_size(axis))]
    return lax.ppermute(value, axis, pairs)


def rms_scale(features):
    return features * lax.rsqrt(jnp.mean(features * features, axis=-1, keepdims=True) + epsilon)


def project(rows_in, matrix):
    return jnp.einsum("...d,dk->...k", rows_in, matrix, preferred_element_type=jnp.float32)


def space_attend(queries, key_rows, value_rows):
    head_count = queries.shape[-1] // HEAD_DIM
    split_dims = queries.shape[:-1] + (head_count, HEAD_DIM)
    scores = jnp.einsum(
        "...qhd,...khd->...hqk",
        queries.reshape(split_dims),
        key_rows.reshape(split_dims),
        preferred_element_type=jnp.float32,
    ) * HEAD_DIM ** (-0.5)
    scores = scores - jnp.max(scores, axis=-1, keepdims=True)
    exponent = jnp.exp(scores)
    soft_weights = (exponent / jnp.sum(exponent, axis=-1, keepdims=True)).astype(jnp.bfloat16)
    result = jnp.einsum(
        "...hqk,...khd->...qhd",
        soft_weights,
        value_rows.reshape(split_dims),
        preferred_element_type=jnp.float32,
    )
    return result.astype(jnp.bfloat16).reshape(queries.shape)


def time_attend(queries, key_rows, value_rows):
    head_count = queries.shape[-1] // HEAD_DIM
    split_dims = queries.shape[:-1] + (head_count, HEAD_DIM)
    scores = jnp.einsum(
        "...fxhd,...gxhd->...xhfg",
        queries.reshape(split_dims),
        key_rows.reshape(split_dims),
        preferred_element_type=jnp.float32,
    ) * HEAD_DIM ** (-0.5)
    scores = scores - jnp.max(scores, axis=-1, keepdims=True)
    exponent = jnp.exp(scores)
    soft_weights = (exponent / jnp.sum(exponent, axis=-1, keepdims=True)).astype(jnp.bfloat16)
    result = jnp.einsum(
        "...xhfg,...gxhd->...fxhd",
        soft_weights,
        value_rows.reshape(split_dims),
        preferred_element_type=jnp.float32,
    )
    return result.astype(jnp.bfloat16).reshape(queries.shape)


def time_core(embedding_rows, query_weight, key_weight, value_weight, out_weight):
    normed = rms_scale(embedding_rows).astype(jnp.bfloat16)
    queries = project(normed, query_weight).astype(jnp.bfloat16)
    key_rows = project(normed, key_weight).astype(jnp.bfloat16)
    value_rows = project(normed, value_weight).astype(jnp.bfloat16)
    return project(time_attend(queries, key_rows, value_rows), out_weight)


def student_network(
    embedding_rows,
    query_weight,
    key_weight,
    value_weight,
    out_weight,
    down_query,
    query_up_map,
    down_value,
    value_up_map,
):
    normed = rms_scale(embedding_rows).astype(jnp.bfloat16)
    low_query = project(normed, down_query).astype(jnp.bfloat16)
    low_value = project(normed, down_value).astype(jnp.bfloat16)
    queries = (project(normed, query_weight) + project(low_query, query_up_map)).astype(
        jnp.bfloat16
    )
    key_rows = project(normed, key_weight).astype(jnp.bfloat16)
    value_rows = (project(normed, value_weight) + project(low_value, value_up_map)).astype(
        jnp.bfloat16
    )
    return project(time_attend(queries, key_rows, value_rows), out_weight)


def on_device(
    clean,
    noise,
    timestep,
    guidance,
    condition_vector,
    empty_prompt_vector,
    timestep_direction,
    spatial_query_key_value,
    spatial_output_weight,
    temporal_query_key_value,
    temporal_output_weight,
    adapter_down_maps,
    adapter_up_maps,
):
    moment = timestep[0]
    strength = guidance[0]
    pair_side = lax.axis_index("cfg")
    noisy_rows = (
        (1.0 - moment) * clean.astype(jnp.float32) + moment * noise.astype(jnp.float32)
    ).astype(jnp.bfloat16)
    shifted = noisy_rows.astype(jnp.float32) + moment * timestep_direction.astype(jnp.float32)
    embeds = jnp.where(pair_side == 0, condition_vector, empty_prompt_vector)[None]
    branch_count = embeds.shape[0]
    entries = shifted[None] + embeds.astype(jnp.float32)[:, None, None, :]
    normed = rms_scale(entries).astype(jnp.bfloat16)
    triple = jnp.einsum(
        "bfpd,jdk->jbfpk",
        normed,
        lax.all_gather(spatial_query_key_value, ("cfg", "seq"), axis=2, tiled=True),
        preferred_element_type=jnp.float32,
    ).astype(jnp.bfloat16)
    attended = space_attend(triple[0], triple[1], triple[2])
    partial_value = jnp.einsum(
        "bfpk,kd->bfpd",
        attended,
        lax.all_gather(spatial_output_weight, ("cfg", "seq"), axis=0, tiled=True),
        preferred_element_type=jnp.float32,
    )
    layer_one = (entries + partial_value).astype(jnp.bfloat16)
    frame_count = layer_one.shape[1]
    position_count = layer_one.shape[2]
    width = layer_one.shape[3]
    stacked = jnp.concatenate([layer_one, noisy_rows[None]], axis=0).reshape(
        branch_count + 1, frame_count, 2, position_count // 2, width
    )
    regrouped = lax.all_to_all(stacked, "seq", split_axis=3, concat_axis=1, tiled=True)
    frames = regrouped.shape[1]
    local_rows = regrouped.shape[3]
    teacher_in = regrouped[:branch_count].reshape(branch_count, frames, 2 * local_rows, width)
    noisy_local = regrouped[branch_count]
    time_qkv, time_out = (
        lax.all_gather(temporal_query_key_value, ("cfg", "seq"), axis=2, tiled=True),
        lax.all_gather(temporal_output_weight, ("cfg", "seq"), axis=0, tiled=True),
    )
    teacher_part = time_core(
        teacher_in.astype(jnp.float32), time_qkv[0], time_qkv[1], time_qkv[2], time_out
    )
    velocity = (
        (teacher_in.astype(jnp.float32) + teacher_part)
        .astype(jnp.bfloat16)
        .reshape(branch_count, frames, 2, local_rows, width)
    )
    own_velocity = velocity[0]
    own_half = lax.dynamic_index_in_dim(own_velocity, pair_side, 1, keepdims=False)
    outgoing = lax.dynamic_index_in_dim(own_velocity, 1 - pair_side, 1, keepdims=False)
    other_half = partner(outgoing, "cfg", 0)
    is_first = pair_side == 0
    cond_velocity = jnp.where(is_first, own_half, other_half)
    uncond_velocity = jnp.where(is_first, other_half, own_half)
    student_noisy = lax.dynamic_index_in_dim(noisy_local, pair_side, 1, keepdims=False)
    query_up_map = adapter_up_maps[0]
    value_up_map = adapter_up_maps[1]
    uncond_float = uncond_velocity.astype(jnp.float32)
    guided = (uncond_float + strength * (cond_velocity.astype(jnp.float32) - uncond_float)).astype(
        jnp.bfloat16
    )
    student_in = (
        student_noisy.astype(jnp.float32)
        + moment * timestep_direction.astype(jnp.float32)
        + condition_vector.astype(jnp.float32)
    )

    def student_map(embedding_rows):
        return student_network(
            embedding_rows,
            time_qkv[0],
            time_qkv[1],
            time_qkv[2],
            time_out,
            adapter_down_maps[0],
            query_up_map,
            adapter_down_maps[1],
            value_up_map,
        )

    partial_value, tangent_part = jax.jvp(student_map, (student_in,), (guided.astype(jnp.float32),))
    primal = (student_in + partial_value).astype(jnp.bfloat16)
    tangent = (guided.astype(jnp.float32) + tangent_part).astype(jnp.bfloat16)
    returned = lax.all_to_all(
        jnp.stack([primal, tangent]), "seq", split_axis=1, concat_axis=2, tiled=True
    )
    return (returned[0], returned[1])


def solution(mesh):
    return jax.shard_map(
        on_device,
        mesh=mesh,
        in_specs=(
            P(("clip", "seq"), None, None),
            P(("clip", "seq"), None, None),
            P("clip"),
            P("clip"),
            P("clip"),
            P(),
            P(),
            P(None, None, ("cfg", "seq")),
            P(("cfg", "seq"), None),
            P(None, None, ("cfg", "seq")),
            P(("cfg", "seq"), None),
            P(),
            P(),
        ),
        out_specs=(P(("clip", "seq"), "cfg", None), P(("clip", "seq"), "cfg", None)),
        check_vma=False,
    )
```

profile of v0, /device:TPU:1, one launch (start us, length us, event | category | flops | bytes accessed | tf_op | source)
XLA Modules:
  0.0 709.1 jit_solution(14930948228672094972)
XLA Ops:
  15.2 113.6 %all-gather.11.cloned.1.call-done = bf16[128,9,1152]{2,1,0:T(8,128)(2,1)} async-done(((bf16[1,9,1152]{2,1,0:T(8,128)(2,1)}), bf16[128,9,1152]{2,1,0:T(8,128)(2,1)}) %all-gather.11.cloned.1.call-update) | async-done | bytes 2654224 | tf_op jit(solution)/shard_map/all_gather | solution.py:136
  128.7 4.3 reshape.305
  133.1 113.3 %all-gather.13.cloned.1.call-done = bf16[128,9,1152]{2,1,0:T(8,128)(2,1)} async-done(((bf16[1,9,1152]{2,1,0:T(8,128)(2,1)}), bf16[128,9,1152]{2,1,0:T(8,128)(2,1)}) %all-gather.13.cloned.1.call-update) | async-done | bytes 2654224 | tf_op jit(solution)/shard_map/all_gather | solution.py:153
  246.4 5.7 reshape.316
  252.2 127.7 %all-gather.7.cloned.1.call-done = bf16[3,1152,1152]{1,0,2:T(4,128)(2,1)} async-done(((bf16[3,1152,9]{1,0,2:T(4,128)(2,1)}), bf16[3,1152,1152]{1,0,2:T(4,128)(2,1)}) %all-gather.7.cloned.1.call-update) | async-done | bytes 7962640 | tf_op jit(solution)/shard_map/all_gather | solution.py:129
  379.8 6.6 fusion.10
  393.0 4.9 fusion.164
  397.9 2.8 fusion.61
  402.4 2.6 pad_maximum_fusion
  405.0 8.0 %all-to-all-start = ((bf16[2,1,2,128,1152]{4,2,0,1,3:T(2,128)(2,1)}), bf16[2,1,2,128,1152]{4,2,0,1,3:T(2,128)(2,1)}, u32[]{:S(2)}, u32[]{:S(2)}) async-start(bf16[2,1,2,128,1152]{4,2,0,1,3:T(2,128)(2,1)} %pad_maximum_fusion), calls=%async_computation | async-start | bytes 2359296 | tf_op jit(solution)/shard_map/all_to_all | solution.py:146
  413.0 99.1 %all-gather.9.cloned.1.call-done = bf16[3,1152,1152]{1,0,2:T(4,128)(2,1)} async-done(((bf16[3,1152,9]{1,0,2:T(4,128)(2,1)}), bf16[3,1152,1152]{1,0,2:T(4,128)(2,1)}) %all-gather.9.cloned.1.call-update) | async-done | bytes 7962640 | tf_op jit(solution)/shard_map/all_gather | solution.py:152
  512.1 24.1 %fusion.161 = (bf16[1,1152,1152]{1,0,2:T(2,128)(2,1)}, bf16[1,1152,1152]{1,0,2:T(2,128)(2,1)}, bf16[1,1152,1152]{1,0,2:T(2,128)(2,1)}) fusion(bf16[3,1152,1152]{1,0,2:T(4,128)(2,1)} %all-gather.9.cloned.1.call-done), kind=kLoop, calls=%fused_computation.171 | loop fusion | bytes 15925248 | tf_op jit(solution)/shard_map/jvp()/slice | solution.py:186
  536.2 10.9 %copy.107 = bf16[1,1152,1152]{2,1,0:T(8,128)(2,1)S(1)} copy(bf16[1,1152,1152]{1,0,2:T(2,128)(2,1)} %get-tuple-element.11) | data formatting | bytes 5308416
  547.1 12.2 %copy.108 = bf16[1,1152,1152]{2,1,0:T(8,128)(2,1)} copy(bf16[1,1152,1152]{1,0,2:T(2,128)(2,1)} %get-tuple-element.13) | data formatting | bytes 5308416
  559.3 12.2 %copy.106 = bf16[1,1152,1152]{2,1,0:T(8,128)(2,1)} copy(bf16[1,1152,1152]{1,0,2:T(2,128)(2,1)} %get-tuple-element.12) | data formatting | bytes 5308416
  576.0 2.8 reshape.295
  578.8 2.9 fusion.37
  581.7 2.8 reshape.296
  584.5 3.6 fusion.66
  588.2 2.6 fusion.165
  590.7 2.5 slice_convert_fusion
  593.3 2.9 fusion.31
  596.2 3.7 reshape.294
  599.9 3.9 fusion.59
  603.8 2.9 copy.88
  606.7 2.9 reshape.297
  609.6 3.2 fusion.41
  614.4 11.1 %collective-permute-start = (bf16[64,2,1152]{2,0,1:T(8,128)(2,1)}, bf16[64,2,1152]{2,0,1:T(8,128)(2,1)S(1)}, u32[]{:S(2)}, u32[]{:S(2)}) collective-permute-start(bf16[64,2,1152]{2,0,1:T(8,128)(2,1)} %dynamic-slice_bitcast_fusion), channel_id=1, source_target_pairs={{0,128},{128,0},{1,129},{129,1},{2,130},{130,2},{3,131},{131,3},{4... | collective-permute-start | bytes 884744 | tf_op jit(solution)/shard_map/ppermute | solution.py:15
  626.2 5.8 collective-permute-done
  633.3 3.4 fusion.29
  664.5 2.3 fusion.55
  677.1 23.1 %all_to_all.24 = bf16[2,64,2,1152]{3,2,0,1:T(2,128)(2,1)S(1)} all-to-all(bf16[2,64,2,1152]{3,2,0,1:T(2,128)(2,1)S(1)} %copy.98), channel_id=1, replica_groups=mesh['cfg'=2,'seq'=64,'clip'=2] {'seq'}, dimensions={1} | all-to-all | bytes 1179648 | tf_op jit(solution)/shard_map/all_to_all | solution.py:199
  (135 shorter events, 62.8 us)
Async XLA Ops:
  7.2 121.6 %all-gather.11.cloned.1.call-start = ((), (), s32[]{:S(2)}) async-start(), calls=%async_computation.4 | async-start | bytes 4755456 | tf_op jit(solution)/shard_map/all_gather | solution.py:136
  7.9 238.5 %all-gather.13.cloned.1.call-start = ((), (), s32[]{:S(2)}) async-start(), calls=%async_computation.5 | async-start | bytes 4755456 | tf_op jit(solution)/shard_map/all_gather | solution.py:153
  8.6 371.2 %all-gather.7.cloned.1.call-start = ((), (), s32[]{:S(2)}) async-start(), calls=%async_computation.2 | async-start | bytes 10699776 | tf_op jit(solution)/shard_map/all_gather | solution.py:129
  9.4 502.7 %all-gather.9.cloned.1.call-start = ((), (), s32[]{:S(2)}) async-start(), calls=%async_computation.3 | async-start | bytes 10699776 | tf_op jit(solution)/shard_map/all_gather | solution.py:152
  13.8 366.1 %copy-start.15 = (bf16[1,256,1152]{2,1,0:T(8,128)(2,1)}, bf16[1,256,1152]{2,1,0:T(8,128)(2,1)S(1)}, u32[]{:S(2)}) copy-start(bf16[1,256,1152]{2,1,0:T(8,128)(2,1)S(1)} %get-tuple-element.10) | copy-start | bytes 1769476
  393.0 4.9 copy-start.22
  397.9 2.8 copy-start.16
  400.7 1.7 copy-start.14
  405.0 166.5 %all-to-all-start = ((bf16[2,1,2,128,1152]{4,2,0,1,3:T(2,128)(2,1)}), bf16[2,1,2,128,1152]{4,2,0,1,3:T(2,128)(2,1)}, u32[]{:S(2)}, u32[]{:S(2)}) async-start(bf16[2,1,2,128,1152]{4,2,0,1,3:T(2,128)(2,1)} %pad_maximum_fusion), calls=%async_computation | async-start | bytes 2359296 | tf_op jit(solution)/shard_map/all_to_all | solution.py:146
  590.7 2.6 copy-start
  614.4 17.6 %collective-permute-start = (bf16[64,2,1152]{2,0,1:T(8,128)(2,1)}, bf16[64,2,1152]{2,0,1:T(8,128)(2,1)S(1)}, u32[]{:S(2)}, u32[]{:S(2)}) collective-permute-start(bf16[64,2,1152]{2,0,1:T(8,128)(2,1)} %dynamic-slice_bitcast_fusion), channel_id=1, source_target_pairs={{0,128},{128,0},{1,129},{129,1},{2,130},{130,2},{3,131},{131,3},{4... | collective-permute-start | bytes 884744 | tf_op jit(solution)/shard_map/ppermute | solution.py:15
  633.3 3.4 copy-start.9
  633.3 7.7 %copy-start.27 = (f32[64,2]{0,1:T(2,128)}, f32[64,2]{0,1:T(2,128)S(1)}, u32[]{:S(2)}) copy-start(f32[64,2]{0,1:T(2,128)S(1)} %get-tuple-element.23) | copy-start | bytes 1540
  633.3 3.6 copy-start.2
  641.0 2.0 copy-start.1
  644.4 4.3 copy-start.13
  646.7 7.1 copy-start.11
  658.1 2.6 copy-start.7
  658.1 2.6 copy-start.25
  658.5 2.1 copy-start.23
  658.9 2.1 copy-start.29
  660.6 3.9 copy-start.3
  666.8 3.7 copy-start.26
  666.8 3.7 copy-start.32
  670.4 2.0 copy-start.33
  670.4 2.0 copy-start.6
  670.5 2.0 copy-start.8
  670.5 2.1 copy-start.24
  670.5 2.1 copy-start.30
  670.5 2.1 copy-start.34
  672.6 2.2 copy-start.10
  674.8 1.6 copy-start.19
  (9 other events, 10.9 us)
Sparse Core Ops, SparseCore 0:
  11.7 117.0 all-gather.10
  132.4 113.9 all-gather.12
  250.0 129.7 all-gather.6
  383.3 128.7 all-gather.8
where the time goes:
time: 718 us; the launch traced here: 709 us
  waiting for transfers between devices  462 us (64%)
  local copies, waits for them, and re-layouts  116 us (16%)
  matrix products  60.1 us (8%)
  blocking collectives  23.1 us (3%)
  starting transfers between devices  19.3 us (3%)
  between operations  15.8 us (2%)
  other arithmetic  12.3 us (2%)
    all_gather x1, waiting for transfers between devices, on_device(): lax.all_gather(spatial_query_key_value, ('cfg', 'seq'), axis=2, tiled=True)  128 us
    all_gather x1, waiting for transfers between devices, on_device(): lax.all_gather(spatial_output_weight, ('cfg', 'seq'), axis=0, tiled=True)  114 us
    all_gather x1, waiting for transfers between devices, on_device(): lax.all_gather(temporal_output_weight, ('cfg', 'seq'), axis=0, tiled=True)  113 us
    all_gather x1, waiting for transfers between devices, on_device(): lax.all_gather(temporal_query_key_value, ('cfg', 'seq'), axis=2, tiled=True)  99.1 us
    unnamed x75, local copies, waits for them, and re-layouts  48.6 us
    dot_general x16, matrix products, project(): jnp.einsum('...d,dk->...k', rows_in, matrix, preferred_element_type=jnp.f...  29.4 us
    slice x1, local copies, waits for them, and re-layouts, student_map(): time_qkv[0]  24.1 us
    all_to_all x1, blocking collectives, on_device(): lax.all_to_all(jnp.stack([primal, tangent]), 'seq', split_axis=1, concat_...  23.1 us
  transfers between devices with their start and end apart: 6, of which 5 were waited for; matrix products, arithmetic and copies ran while one was open for 14% of the time, Pallas kernels for 0%

commit v1 on v0

v1 whole, which is shorter than its diff:
```python
import functools

import jax
import jax.numpy as jnp
from jax import lax
from jax.experimental import pallas as pl
from jax.experimental.pallas import tpu as pltpu
from jax.sharding import PartitionSpec as P

MESH = pl.DeviceIdType.MESH
HEAD_DIM = 72
PIECE = 9
SCALE = HEAD_DIM ** (-0.5)
epsilon = 1e-06
F32 = jnp.float32
BF16 = jnp.bfloat16

NX, NY, NZ = 4, 4, 8
QKV_ROWS = 32
CHUNK_ROWS = 48


def dot_nt(a, b):
    return lax.dot_general(a, b, (((1,), (1,)), ((), ())), preferred_element_type=F32)


def dot_nn(a, b):
    return lax.dot_general(a, b, (((1,), (0,)), ((), ())), preferred_element_type=F32)


class Copies:
    def __init__(self, send_sem, recv_sem, names):
        self.send_sem, self.recv_sem = send_sem, recv_sem
        self.ids = {name: i for i, name in enumerate(names)}
        self.sent = []

    def _id(self, name):
        return self.ids[name]

    def send(self, name, src, dst, target):
        i = self._id(name)
        copy = pltpu.make_async_remote_copy(
            src_ref=src, dst_ref=dst, send_sem=self.send_sem.at[i], recv_sem=self.recv_sem.at[i],
            device_id=target, device_id_type=MESH,
        )
        copy.start()
        self.sent.append(copy)

    def recv(self, name, dst, target):
        i = self._id(name)
        pltpu.make_async_remote_copy(
            src_ref=dst, dst_ref=dst, send_sem=self.send_sem.at[i], recv_sem=self.recv_sem.at[i],
            device_id=target, device_id_type=MESH,
        ).wait_recv()

    def finish(self):
        for copy in self.sent:
            copy.wait_send()


ALL = slice(None)
LOW, HIGH = pl.ds(0, 2), pl.ds(2, 2)


def copy_names(layer):
    names = [("minor", layer, d) for d in (1, 2, 3)]
    names += [(way, layer, k) for way in ("up", "down") for k in range(4)]
    names += [(way, layer, j) for way in ("right", "left", "fright", "fleft") for j in range(8)]
    return names + [("sib", c, layer, q, j) for c in range(2) for q in range(4) for j in range(8)]


def gather_kernel(layers, chunk_ref, w_ref, send_sem, recv_sem, local_sem):
    cfg, seq, core = lax.axis_index("cfg"), lax.axis_index("seq"), lax.axis_index("clip")
    x = cfg * 2 + seq // 32
    z = (seq % 32) // 4
    y = seq % 4

    def run(color):
        rows = pl.ds(24 * color, 24)
        minor, major = (y, x) if color == 0 else (x, y)

        def device(mj, zz, mn, which=color):
            xx, yy = (mj, mn) if color == 0 else (mn, mj)
            return (xx // 2, (xx % 2) * 32 + zz * 4 + yy, which)

        def block(layer, mj, zz, mn=ALL, own=color):
            xx, yy = (mj, mn) if own == 0 else (mn, mj)
            return w_ref.at[layer, xx, zz, yy, pl.ds(24 * own, 24)]

        def mod4(a):
            return (a + 4) % 4

        def mod8(a):
            return (a + 8) % 8

        sibling = device(major, z, minor, 1 - color)
        up, down = device(major, mod8(z + 1), minor), device(major, mod8(z - 1), minor)
        right, left = device(mod4(major + 1), z, minor), device(mod4(major - 1), z, minor)
        ring = [device(major, z, mod4(minor + d)) for d in (1, 2, 3)]

        barrier = pltpu.get_barrier_semaphore()
        peers = ring + [up, down, right, left, sibling]
        for peer in peers:
            pl.semaphore_signal(barrier, inc=1, device_id=peer, device_id_type=MESH)
        pl.semaphore_wait(barrier, len(peers))

        copies = Copies(send_sem, recv_sem, [n for layer in range(layers) for n in copy_names(layer)])

        for layer in range(layers):
            own = chunk_ref.at[layer, rows]
            here = block(layer, major, z, minor)
            for d in (1, 2, 3):
                copies.send(("minor", layer, d), own, here, ring[d - 1])
            keep = pltpu.make_async_copy(own, here, local_sem.at[layer])
            keep.start()

        def arrived_minor(layer):
            own = chunk_ref.at[layer, rows]
            here = block(layer, major, z, minor)
            pltpu.make_async_copy(own, here, local_sem.at[layer]).wait()
            for d in (1, 2, 3):
                copies.recv(("minor", layer, d), block(layer, major, z, mod4(minor - d)), sibling)

        def spread(layer, j):
            b = block(layer, major, mod8(z + j))
            copies.send(("right", layer, j % 8), b, b, right)
            copies.send(("left", layer, j % 8), b, b, left)
            copies.send(("sib", color, layer, 0, j % 8), b, b, sibling)

        def z_send(layer, k):
            mn_up, mn_down = (ALL, ALL) if k < 3 else (LOW, HIGH)
            b = block(layer, major, mod8(z - k), mn_up)
            copies.send(("up", layer, k), b, b, up)
            b = block(layer, major, mod8(z + k), mn_down)
            copies.send(("down", layer, k), b, b, down)

        def z_recv(layer, k):
            mn_up, mn_down = (ALL, ALL) if k < 3 else (LOW, HIGH)
            copies.recv(("up", layer, k), block(layer, major, mod8(z - 1 - k), mn_up), sibling)
            copies.recv(("down", layer, k), block(layer, major, mod8(z + 1 + k), mn_down), sibling)

        groups = [(0,), (-1, 1), (-2, 2), (-3, 3), (4,)]

        def pass_on(layer, j):
            zz = mod8(z + j)
            copies.recv(("right", layer, j % 8), block(layer, mod4(major - 1), zz), sibling)
            b = block(layer, mod4(major - 1), zz)
            h = block(layer, mod4(major - 1), zz, LOW)
            copies.send(("fright", layer, j % 8), h, h, right)
            copies.send(("sib", color, layer, 1, j % 8), b, b, sibling)
            copies.recv(("left", layer, j % 8), block(layer, mod4(major + 1), zz), sibling)
            b = block(layer, mod4(major + 1), zz)
            h = block(layer, mod4(major + 1), zz, HIGH)
            copies.send(("fleft", layer, j % 8), h, h, left)
            copies.send(("sib", color, layer, 2, j % 8), b, b, sibling)

        def last(layer, j):
            zz = mod8(z + j)
            far = mod4(major + 2)
            copies.recv(("fright", layer, j % 8), block(layer, far, zz, LOW), sibling)
            copies.recv(("fleft", layer, j % 8), block(layer, far, zz, HIGH), sibling)
            b = block(layer, far, zz)
            copies.send(("sib", color, layer, 3, j % 8), b, b, sibling)

        for layer in range(layers):
            arrived_minor(layer)
            for k in range(5):
                if k > 0:
                    z_recv(layer, k - 1)
                if k < 4:
                    z_send(layer, k)
                for j in groups[k]:
                    spread(layer, j)
                if layer > 0:
                    for j in groups[k]:
                        pass_on(layer - 1, j)
        for k in range(5):
            for j in groups[k]:
                pass_on(layers - 1, j)
        for layer in range(layers):
            for k in range(5):
                for j in groups[k]:
                    last(layer, j)

        other = 1 - color
        other_major = y if color == 0 else x
        for layer in range(layers):
            for q, dm in enumerate((0, 3, 1, 2)):
                for k in range(5):
                    for j in groups[k]:
                        copies.recv(
                            ("sib", other, layer, q, j % 8),
                            block(layer, mod4(other_major + dm), mod8(z + j), ALL, other),
                            sibling,
                        )
        copies.finish()

    @pl.when(core == 0)
    def _():
        run(0)

    @pl.when(core == 1)
    def _():
        run(1)


def gather_weights(chunks):
    layers = chunks.shape[0]
    n = layers * len(copy_names(0))
    return pl.pallas_call(
        functools.partial(gather_kernel, layers),
        out_shape=jax.ShapeDtypeStruct((layers, NX, NZ, NY, CHUNK_ROWS, chunks.shape[-1]), BF16),
        in_specs=[pl.BlockSpec(memory_space=pl.ANY)],
        out_specs=pl.BlockSpec(memory_space=pl.ANY),
        scratch_shapes=[
            pltpu.SemaphoreType.DMA((n,)),
            pltpu.SemaphoreType.DMA((n,)),
            pltpu.SemaphoreType.DMA((layers,)),
        ],
        compiler_params=pltpu.CompilerParams(collective_id=0, has_side_effects=True),
        name="weights",
    )(chunks)


def wire_chunk(qkv, out):
    width = out.shape[-1]
    rows = jnp.transpose(qkv, (0, 2, 1)).reshape(3 * PIECE, width)
    zeros = lambda n: jnp.zeros((n, width), BF16)
    return jnp.concatenate([rows, zeros(QKV_ROWS - 3 * PIECE + 2), out, zeros(5)], axis=0)


def lanes(rows):
    return lax.broadcasted_iota(jnp.int32, (rows, 256), 1) % 32


def soft(scores):
    scores = scores - jnp.max(scores, axis=-1, keepdims=True)
    exponent = jnp.exp(scores)
    return exponent / jnp.sum(exponent, axis=-1, keepdims=True)


def head_parts(t):
    q = jnp.where(lanes(t.shape[0]) < PIECE, t, 0.0).astype(BF16)
    k = pltpu.roll(t, 256 - PIECE, 1).astype(BF16)
    return q, k, t.astype(BF16)


def pair_columns(first, second):
    shifted = pltpu.roll(second, 256 - 16, 1)
    return jnp.where(lanes(first.shape[0]) >= 16, first, shifted).astype(BF16)


def pair_weights(w_ref):
    width = w_ref.shape[-1]
    w = w_ref.reshape(16, CHUNK_ROWS, width)
    qkv = [w[8 * i : 8 * i + 8, :QKV_ROWS].reshape(256, width) for i in range(2)]
    out = [w[8 * i : 8 * i + 8, QKV_ROWS:].reshape(8, 1, 16, width) for i in range(2)]
    return qkv, jnp.concatenate([out[1], out[0]], axis=1).reshape(256, width)


def rms(e):
    return e * lax.rsqrt(jnp.mean(e * e, axis=-1, keepdims=True) + epsilon)


def space_kernel(moment_ref, clean_ref, noise_ref, dir_ref, emb_ref, w_ref, out_ref, entry, normed, acc):
    step = pl.program_id(0)

    @pl.when(step == 0)
    def _():
        t = moment_ref[0]
        noisy = ((1.0 - t) * clean_ref[...].astype(F32) + t * noise_ref[...].astype(F32)).astype(BF16)
        e = noisy.astype(F32) + t * dir_ref[...] + emb_ref[...]
        entry[...] = e
        normed[...] = rms(e).astype(BF16)
        acc[...] = jnp.zeros_like(acc)

    qkv, out_w = pair_weights(w_ref)
    mixed = []
    for i in range(2):
        t = dot_nt(normed[...], qkv[i])
        q, k, v = head_parts(t)
        weights = soft(dot_nt(q, k) * SCALE).astype(BF16)
        mixed.append(dot_nn(weights, v))
    acc[...] += dot_nn(pair_columns(*mixed), out_w)

    @pl.when(step == pl.num_programs(0) - 1)
    def _():
        out_ref[...] = (entry[...] + acc[...]).astype(BF16)


def w_spec(layer, width, steps=8):
    return pl.BlockSpec(
        (None, None, None, 16, CHUNK_ROWS, width),
        lambda i, *_: (layer, (i % 8) // 2, (i % 8) % 2, 0, 0, 0),
    )


def full(shape):
    return pl.BlockSpec(shape, lambda i: (0,) * len(shape))


def space_layer(moment, clean, noise, direction, emb, weights):
    rows, width = clean.shape
    return pl.pallas_call(
        space_kernel,
        grid=(8,),
        out_shape=jax.ShapeDtypeStruct((rows, width), BF16),
        in_specs=[
            pl.BlockSpec(memory_space=pltpu.SMEM),
            full((rows, width)),
            full((rows, width)),
            full((1, width)),
            full((1, width)),
            w_spec(0, width),
        ],
        out_specs=full((rows, width)),
        scratch_shapes=[
            pltpu.VMEM((rows, width), F32),
            pltpu.VMEM((rows, width), BF16),
            pltpu.VMEM((rows, width), F32),
        ],
        name="space",
    )(moment, clean, noise, direction, emb, weights)


def same_position(rows):
    a = lax.broadcasted_iota(jnp.int32, (rows, rows), 0)
    b = lax.broadcasted_iota(jnp.int32, (rows, rows), 1)
    return a % 2 == b % 2


NEG = -1e30


def time_kernel(
    scal_ref, teach_ref, noisy_ref, dir_ref, cond_ref, down_ref, up_ref, w_ref,
    out_ref, tan_ref, normed, student, entry, guide, acc,
):
    step = pl.program_id(0)
    half = noisy_ref.shape[0]
    width = noisy_ref.shape[1]

    @pl.when(step == 0)
    def _():
        normed[...] = rms(teach_ref[...].astype(F32)).astype(BF16)
        acc[...] = jnp.zeros_like(acc)

    @pl.when(step == 8)
    def _():
        velocity = (teach_ref[...].astype(F32) + acc[...]).astype(BF16).astype(F32)
        cond, uncond = velocity[:half], velocity[half:]
        guided = (uncond + scal_ref[1] * (cond - uncond)).astype(BF16).astype(F32)
        guide[...] = guided
        e = noisy_ref[...].astype(F32) + scal_ref[0] * dir_ref[...] + cond_ref[...]
        entry[...] = e
        scale = lax.rsqrt(jnp.mean(e * e, axis=-1, keepdims=True) + epsilon)
        cross = jnp.mean(e * guided, axis=-1, keepdims=True)
        student[:half, :width] = (e * scale).astype(BF16)
        student[half:, :width] = (scale * (guided - e * (scale * scale * cross))).astype(BF16)
        student[:, width:] = dot_nn(student[:, :width], down_ref[...]).astype(BF16)
        acc[...] = jnp.zeros_like(acc)

    qkv, out_w = pair_weights(w_ref)

    @pl.when(step < 8)
    def _():
        mixed = []
        same = same_position(half)
        for i in range(2):
            q, k, v = head_parts(dot_nt(normed[...], qkv[i]))
            parts = []
            for b in range(2):
                r = slice(b * half, (b + 1) * half)
                scores = jnp.where(same, dot_nt(q[r], k[r]) * SCALE, NEG)
                parts.append(dot_nn(soft(scores).astype(BF16), v[r]))
            mixed.append(jnp.concatenate(parts, axis=0))
        acc[...] += dot_nn(pair_columns(*mixed), out_w)

    @pl.when(step >= 8)
    def _():
        mixed = []
        same = same_position(half)
        for i in range(2):
            t = dot_nt(student[:, :width], qkv[i]) + dot_nt(student[:, width:], up_ref[i])
            q, k, v = head_parts(t)
            s = dot_nt(q, k) * SCALE
            weights = soft(jnp.where(same, s[:half, :half], NEG))
            ds = s[:half, half:] + s[half:, :half]
            dw = weights * (ds - jnp.sum(weights * ds, axis=-1, keepdims=True))
            weights, dw = weights.astype(BF16), dw.astype(BF16)
            top = jnp.concatenate([weights, jnp.zeros_like(weights)], axis=1)
            low = jnp.concatenate([dw, weights], axis=1)
            mixed.append(dot_nn(jnp.concatenate([top, low], axis=0), v))
        acc[...] += dot_nn(pair_columns(*mixed), out_w)

    @pl.when(step == pl.num_programs(0) - 1)
    def _():
        out_ref[...] = (entry[...] + acc[:half]).astype(BF16)
        tan_ref[...] = (guide[...] + acc[half:]).astype(BF16)


def time_layer(scalars, teach, noisy, direction, cond, down, up, weights):
    half, width = noisy.shape
    return pl.pallas_call(
        time_kernel,
        grid=(16,),
        out_shape=[jax.ShapeDtypeStruct((half, width), BF16)] * 2,
        in_specs=[
            pl.BlockSpec(memory_space=pltpu.SMEM),
            full((2 * half, width)),
            full((half, width)),
            full((1, width)),
            full((1, width)),
            full(down.shape),
            pl.BlockSpec((None, 2, 256, 128), lambda i: (jnp.maximum(i - 8, 0), 0, 0, 0)),
            w_spec(1, width),
        ],
        out_specs=[full((half, width))] * 2,
        scratch_shapes=[
            pltpu.VMEM((2 * half, width), BF16),
            pltpu.VMEM((2 * half, width + 128), BF16),
            pltpu.VMEM((half, width), F32),
            pltpu.VMEM((half, width), F32),
            pltpu.VMEM((2 * half, width), F32),
        ],
        name="time",
    )(scalars, teach, noisy, direction, cond, down, up, weights)


def tangled_up(up_maps):
    rank, width = up_maps.shape[1], up_maps.shape[2]
    rows = jnp.transpose(up_maps, (0, 2, 1)).reshape(2, width // PIECE, PIECE, rank)
    query = jnp.pad(rows[0], ((0, 0), (0, QKV_ROWS - PIECE), (0, 0)))
    value = jnp.pad(rows[1], ((0, 0), (2 * PIECE, QKV_ROWS - 3 * PIECE), (0, 0)))
    return jnp.concatenate([query, value], axis=-1).reshape(8, 2, 256, 2 * rank)


def on_device(
    clean, noise, timestep, guidance, condition_vector, empty_prompt_vector, timestep_direction,
    spatial_query_key_value, spatial_output_weight, temporal_query_key_value, temporal_output_weight,
    adapter_down_maps, adapter_up_maps,
):
    side = lax.axis_index("cfg")
    width = clean.shape[-1]
    positions = clean.shape[1]
    moment = timestep[0]
    chunks = jnp.stack(
        [
            wire_chunk(spatial_query_key_value, spatial_output_weight),
            wire_chunk(temporal_query_key_value, temporal_output_weight),
        ]
    )
    weights = gather_weights(chunks)
    weights = weights.reshape(2, NX, 2, 16, CHUNK_ROWS, width)
    direction = timestep_direction.astype(F32)[None]
    cond = condition_vector.astype(F32)[None]
    emb = jnp.where(side == 0, condition_vector, empty_prompt_vector).astype(F32)[None]
    layer_one = space_layer(timestep, clean[0], noise[0], direction, emb, weights)
    teach = lax.all_to_all(
        layer_one.reshape(positions // 2, 2, width), ("cfg", "seq"), split_axis=0, concat_axis=0, tiled=True
    ).reshape(positions, width)
    half = positions // 2
    own = lambda a: lax.dynamic_slice_in_dim(a[0], side * half, half, 0).astype(F32)
    noisy = ((1.0 - moment) * own(clean) + moment * own(noise)).astype(BF16)
    noisy = lax.all_to_all(
        noisy.reshape(half // 2, 2, width), "seq", split_axis=0, concat_axis=0, tiled=True
    ).reshape(half, width)
    down = jnp.transpose(adapter_down_maps, (1, 0, 2)).reshape(width, -1)
    scalars = jnp.concatenate([timestep, guidance])
    primal, tangent = time_layer(
        scalars, teach, noisy, direction, cond, down, tangled_up(adapter_up_maps), weights
    )
    returned = lax.all_to_all(
        jnp.stack([primal, tangent]).reshape(2, half // 2, 2, width), "seq", split_axis=1, concat_axis=1, tiled=True
    ).reshape(2, 1, half, width)
    return returned[0], returned[1]


def solution(mesh):
    return jax.shard_map(
        on_device,
        mesh=mesh,
        in_specs=(
            P(("clip", "seq"), None, None),
            P(("clip", "seq"), None, None),
            P("clip"),
            P("clip"),
            P("clip"),
            P(),
            P(),
            P(None, None, ("cfg", "seq")),
            P(("cfg", "seq"), None),
            P(None, None, ("cfg", "seq")),
            P(("cfg", "seq"), None),
            P(),
            P(),
        ),
        out_specs=(P(("clip", "seq"), "cfg", None), P(("clip", "seq"), "cfg", None)),
        check_vma=False,
    )
```

time: 718 us -> 244 us (0.34)
  waiting for transfers between devices: 462 us -> 12.9 us
  Pallas kernels: 0 us -> 160 us
  local copies, waits for them, and re-layouts: 116 us -> 13.3 us
  matrix products: 60.1 us -> 0 us
  between operations: 15.8 us -> 2.22 us
  other arithmetic: 12.3 us -> 4.89 us
    all_gather x4 -> x0, waiting for transfers between devices: 454 us -> none  [the longest x1 128 us: on_device(): lax.all_gather(spatial_query_key_value, ('cfg', 'seq'), axis=2, tiled=True)]
    pallas_call x0 -> x3, Pallas kernels: none -> 160 us  [the longest x1 87.9 us: gather_weights(): pl.pallas_call(functools.partial(gather_kernel, layers), out_shape=jax.Sh...]
    dot_general x27 -> x0, matrix products: 52.7 us -> none  [the longest x16 29.4 us: project(): jnp.einsum('...d,dk->...k', rows_in, matrix, preferred_element_type=jnp.f...]
    unnamed x75 -> x18, local copies, waits for them, and re-layouts: 48.6 us -> 0.04 us
    slice x5 -> x3, local copies, waits for them, and re-layouts: 30.6 us -> 0.46 us  [the longest x2 0.24 us: tangled_up(): query = jnp.pad(rows[0], ((0, 0), (0, QKV_ROWS - PIECE), (0, 0)))]
    all_to_all x1 -> x2, starting transfers between devices: 8.03 us -> 24.7 us  [the longest x1 13.6 us: on_device(): lax.all_to_all(noisy.reshape(half // 2, 2, width), 'seq', split_axis=0, c...]
    all_to_all x1 -> x2, waiting for transfers between devices: 0.01 us -> 12.9 us  [the longest x1 12.9 us: on_device(): lax.all_to_all(layer_one.reshape(positions // 2, 2, width), ('cfg', 'seq'...]
    ppermute x1 -> x0, starting transfers between devices: 11.1 us -> none  [partner(): return lax.ppermute(value, axis, pairs)]
  transfers between devices with their start and end apart: 6 -> 2, of which waited for: 5 -> 1; matrix products, arithmetic and copies ran while one was open for 14% -> 4% of each run, Pallas kernels for 0% -> 46%
where the time goes in v1:
time: 244 us; the launch traced here: 241 us
  Pallas kernels  160 us (66%)
  starting transfers between devices  24.7 us (10%)
  blocking collectives  23 us (9%)
  local copies, waits for them, and re-layouts  13.3 us (5%)
  waiting for transfers between devices  12.9 us (5%)
  other arithmetic  4.89 us (2%)
    pallas_call x1, Pallas kernels, gather_weights(): pl.pallas_call(functools.partial(gather_kernel, layers), out_shape=jax.Sh...  87.9 us
    pallas_call x1, Pallas kernels, time_layer(): pl.pallas_call(time_kernel, grid=(16,), out_shape=[jax.ShapeDtypeStruct((...  50.1 us
    all_to_all x1, blocking collectives, on_device(): lax.all_to_all(jnp.stack([primal, tangent]).reshape(2, half // 2, 2, widt...  23 us
    pallas_call x1, Pallas kernels, space_layer(): pl.pallas_call(space_kernel, grid=(8,), out_shape=jax.ShapeDtypeStruct((r...  22.3 us
    all_to_all x1, starting transfers between devices, on_device(): lax.all_to_all(noisy.reshape(half // 2, 2, width), 'seq', split_axis=0, c...  13.6 us
    all_to_all x1, waiting for transfers between devices, on_device(): lax.all_to_all(layer_one.reshape(positions // 2, 2, width), ('cfg', 'seq'...  12.9 us
    all_to_all x1, starting transfers between devices, on_device(): lax.all_to_all(layer_one.reshape(positions // 2, 2, width), ('cfg', 'seq'...  11.1 us
  transfers between devices with their start and end apart: 2, of which 1 were waited for; matrix products, arithmetic and copies ran while one was open for 4% of the time, Pallas kernels for 46%

profile of v1, /device:TPU:1, one launch (start us, length us, event | category | flops | bytes accessed | tf_op | source)
XLA Modules:
  0.0 241.4 jit_solution(14866330117364392531)
XLA Ops:
  1.4 1.2 add_convert_fusion
  2.6 0.8 convert_element_type.27
  3.4 13.6 %all-to-all-start.1 = ((bf16[64,2,1152]{2,1,0:T(2,128)(2,1)}), bf16[64,2,1152]{2,1,0:T(2,128)(2,1)S(1)}, u32[]{:S(2)}, u32[]{:S(2)}) async-start(bf16[64,2,1152]{2,1,0:T(2,128)(2,1)} %convert_element_type.27), calls=%async_computation.1 | async-start | bytes 589824 | tf_op jit(solution)/shard_map/all_to_all | solution.py:465
  17.0 0.1 pad.23.clone
  17.1 0.1 pad.21.clone
  17.2 0.6 reshape.64.dir_ref
  17.8 0.6 reshape.65.emb_ref
  18.5 0.1 maximum_bitcast_fusion
  18.7 0.7 pad_maximum_fusion.1.chunk_ref
  19.4 87.9 %weights.1 = bf16[2,4,8,4,48,1152]{5,4,3,2,1,0:T(8,128)(2,1)} custom-call(bf16[2,48,1152]{2,1,0:T(8,128)(2,1)} %pad_maximum_fusion.1.chunk_ref), custom_call_target="tpu_custom_call" | custom-call | tf_op jit(solution)/shard_map/weights/pallas_call | solution.py:210
  107.3 22.3 %space.1 = bf16[256,1152]{1,0:T(8,128)(2,1)} custom-call(f32[1]{0:T(128)} %copy.32.moment_ref, bf16[256,1152]{1,0:T(8,128)(2,1)} %bitcast.26, bf16[256,1152]{1,0:T(8,128)(2,1)} %bitcast.27, f32[1,1152]{1,0:T(1,128)} %reshape.64.dir_ref, f32[1,1152]{1,0:T(1,128)} %reshape.65.emb_ref, bf16[2,4,2,16,48,1152]{5,4,3,2,1,0:T(8,128)(2,1)} %bitcast.23), custom_call_target="tpu_custom_call" | custom-call | tf_op jit(solution)/shard_map/space/pallas_call | solution.py:304
  129.6 2.7 %reshape.59 = bf16[128,2,1152]{2,1,0:T(2,128)(2,1)} reshape(bf16[256,1152]{1,0:T(8,128)(2,1)} %space.1) | data formatting | bytes 1179648 | tf_op jit(solution)/shard_map/reshape | solution.py:460
  132.3 11.1 %all-to-all-start = ((bf16[128,2,1152]{2,1,0:T(2,128)(2,1)}), bf16[128,2,1152]{2,1,0:T(2,128)(2,1)S(1)}, u32[]{:S(2)}, u32[]{:S(2)}) async-start(bf16[128,2,1152]{2,1,0:T(2,128)(2,1)} %reshape.59), calls=%async_computation | async-start | bytes 1179648 | tf_op jit(solution)/shard_map/all_to_all | solution.py:459
  143.4 0.6 reshape.66.cond_ref
  144.7 0.9 copy.29.down_ref
  145.6 0.2 copy.27
  145.8 0.1 squeeze.26
  145.9 0.2 copy.28
  146.2 0.1 squeeze.27
  146.3 0.6 pad_maximum_fusion.2.scal_ref
  146.9 1.5 fusion.2
  148.4 0.8 reshape.61.noisy_ref
  149.2 12.9 %all-to-all-done = bf16[128,2,1152]{2,1,0:T(2,128)(2,1)S(1)} async-done(((bf16[128,2,1152]{2,1,0:T(2,128)(2,1)}), bf16[128,2,1152]{2,1,0:T(2,128)(2,1)S(1)}, u32[]{:S(2)}, u32[]{:S(2)}) %all-to-all-start) | async-done | bytes 589856 | tf_op jit(solution)/shard_map/all_to_all | solution.py:459
  162.2 1.1 reshape.60.teach_ref
  163.3 50.1 %time.1 = (bf16[128,1152]{1,0:T(8,128)(2,1)}, bf16[128,1152]{1,0:T(8,128)(2,1)}) custom-call(f32[2]{0:T(128)} %pad_maximum_fusion.2.scal_ref, bf16[256,1152]{1,0:T(8,128)(2,1)} %reshape.60.teach_ref, bf16[128,1152]{1,0:T(8,128)(2,1)} %reshape.61.noisy_ref, f32[1,1152]{1,0:T(1,128)} %reshape.64.dir_ref, f32[1,1152]{1,0:T(1,128)} %reshape.66.cond_ref, ...), custom_call_target="tpu_custom_call" | custom-call | tf_op jit(solution)/shard_map/time/pallas_call | solution.py:404
  213.4 1.1 stack.21
  214.4 1.1 stack.22
  215.5 0.8 pad_maximum_fusion
  216.3 23.0 %all_to_all.15 = bf16[2,64,2,1152]{3,2,0,1:T(2,128)(2,1)S(1)} all-to-all(bf16[2,64,2,1152]{3,2,0,1:T(2,128)(2,1)S(1)} %pad_maximum_fusion), channel_id=1, replica_groups=mesh['cfg'=2,'seq'=64,'clip'=2] {'seq'}, dimensions={1} | all-to-all | bytes 1179648 | tf_op jit(solution)/shard_map/all_to_all | solution.py:473
  239.3 0.4 fusion.3
  239.7 0.8 squeeze.29
  240.6 0.8 squeeze.28
  (27 shorter events, 0.2 us)
Async XLA Ops:
  0.6 16.5 %copy-start.7 = (bf16[1152]{0:T(1024)(128)(2,1)S(1)}, bf16[1152]{0:T(1024)(128)(2,1)}, u32[]{:S(2)}) copy-start(bf16[1152]{0:T(1024)(128)(2,1)} %param.19) | copy-start | bytes 6916
  0.6 17.1 %copy-start.6 = (bf16[1152]{0:T(1024)(128)(2,1)S(1)}, bf16[1152]{0:T(1024)(128)(2,1)}, u32[]{:S(2)}) copy-start(bf16[1152]{0:T(1024)(128)(2,1)} %param.17) | copy-start | bytes 6916
  0.7 17.1 %copy-start.8 = (bf16[1152]{0:T(1024)(128)(2,1)S(1)}, bf16[1152]{0:T(1024)(128)(2,1)}, u32[]{:S(2)}) copy-start(bf16[1152]{0:T(1024)(128)(2,1)} %param.18) | copy-start | bytes 6916
  0.7 17.7 %copy-start.2 = (bf16[3,1152,9]{1,0,2:T(4,128)(2,1)S(1)}, bf16[3,1152,9]{1,0,2:T(4,128)(2,1)}, u32[]{:S(2)}) copy-start(bf16[3,1152,9]{1,0,2:T(4,128)(2,1)} %param.20) | copy-start | bytes 186628
  0.7 17.8 %copy-start.3 = (bf16[3,1152,9]{1,0,2:T(4,128)(2,1)S(1)}, bf16[3,1152,9]{1,0,2:T(4,128)(2,1)}, u32[]{:S(2)}) copy-start(bf16[3,1152,9]{1,0,2:T(4,128)(2,1)} %param.22) | copy-start | bytes 186628
  0.7 17.8 %copy-start.5 = (bf16[9,1152]{1,0:T(8,128)(2,1)S(1)}, bf16[9,1152]{1,0:T(8,128)(2,1)}, u32[]{:S(2)}) copy-start(bf16[9,1152]{1,0:T(8,128)(2,1)} %param.23) | copy-start | bytes 62212
  0.7 17.8 %copy-start.4 = (bf16[9,1152]{1,0:T(8,128)(2,1)S(1)}, bf16[9,1152]{1,0:T(8,128)(2,1)}, u32[]{:S(2)}) copy-start(bf16[9,1152]{1,0:T(8,128)(2,1)} %param.21) | copy-start | bytes 62212
  3.4 128.9 %all-to-all-start.1 = ((bf16[64,2,1152]{2,1,0:T(2,128)(2,1)}), bf16[64,2,1152]{2,1,0:T(2,128)(2,1)S(1)}, u32[]{:S(2)}, u32[]{:S(2)}) async-start(bf16[64,2,1152]{2,1,0:T(2,128)(2,1)} %convert_element_type.27), calls=%async_computation.1 | async-start | bytes 589824 | tf_op jit(solution)/shard_map/all_to_all | solution.py:465
  129.6 15.1 %copy-start = (bf16[2,1152,64]{1,2,0:T(8,128)(2,1)S(1)}, bf16[2,1152,64]{1,2,0:T(8,128)(2,1)}, u32[]{:S(2)}) copy-start(bf16[2,1152,64]{1,2,0:T(8,128)(2,1)} %param.24) | copy-start | bytes 884740
  129.6 16.0 %copy-start.1 = (bf16[2,64,1152]{2,1,0:T(8,128)(2,1)S(1)}, bf16[2,64,1152]{2,1,0:T(8,128)(2,1)}, u32[]{:S(2)}) copy-start(bf16[2,64,1152]{2,1,0:T(8,128)(2,1)} %param.25) | copy-start | bytes 884740
  132.3 29.9 %all-to-all-start = ((bf16[128,2,1152]{2,1,0:T(2,128)(2,1)}), bf16[128,2,1152]{2,1,0:T(2,128)(2,1)S(1)}, u32[]{:S(2)}, u32[]{:S(2)}) async-start(bf16[128,2,1152]{2,1,0:T(2,128)(2,1)} %reshape.59), calls=%async_computation | async-start | bytes 1179648 | tf_op jit(solution)/shard_map/all_to_all | solution.py:459
